TPU v7x, 256 devices: a whole 4x4x8 slice. The times are simulated.
256 devices in a mesh: gx: 16 (over z, core), gy: 4 (over x), member: 4 (over y).
Axes of the slice: x: 4, y: 4, z: 8, core: 2. Of those that a mesh axis runs over, the one named last changes fastest.
Arguments:
- density: float32 [4, 64, 128, 256], P('member', 'gx', 'gy'), may hold values from 0.5 to 1.5
- velocity: float32 [4, 3, 64, 128, 256], P('member', None, 'gx', 'gy'), may hold values from -0.5 to 0.5
- pressure: float32 [4, 64, 128, 256], P('member', 'gx', 'gy'), may hold values from 0.5 to 1.5
- start_block: float32 [4, 128, 16], P('member'), may hold values from -6 to 6
- test_vectors: float32 [32, 64, 128], P('gx', 'gy'), may hold values from -48 to 48
Outputs:
- state_next: float32 [4, 5, 64, 128, 256], P('member', None, 'gx', 'gy')
- projected: float32 [32, 64, 128], P('gx', 'gy')
All inputs are finite; a program needn't handle non-finite values.
Results may differ from a plain program's by a relative error of at most 0.00013.
Values sent between devices are 32-bit elements; how exact they have to be, the bound alone decides.
A program may use at most 64 MiB of HBM per device.

v0:
```python
import jax
import jax.numpy as jnp
from jax import lax
from jax.sharding import PartitionSpec as P

HEAT_RATIO = 1.4
TIME_STEP = 0.08
PRECISE = lax.Precision.HIGHEST


def padded(block, sides, width):
    for axis, dim in sides:
        count = lax.axis_size(axis)
        forward = [(i, i + 1) for i in range(count - 1)]
        forward.append((count - 1, 0))
        backward = [(target, source) for source, target in forward]
        low = lax.ppermute(
            lax.slice_in_dim(block, block.shape[dim] - width, None, axis=dim), axis, forward
        )
        high = lax.ppermute(lax.slice_in_dim(block, 0, width, axis=dim), axis, backward)
        block = jnp.concatenate([low, block, high], axis=dim)
    return block


def cut(values, dimension, start_at, stop_at):
    return lax.slice_in_dim(values, start_at, stop_at, axis=dimension)


def conserved(density, velocity, pressure):
    momentum = density[None] * velocity
    energy = pressure / (HEAT_RATIO - 1.0) + 0.5 * density * jnp.sum(velocity * velocity, axis=0)
    return jnp.concatenate([density[None], momentum, energy[None]], axis=0)


def primitive(fields):
    velocity = fields[1:4] / fields[0]
    kinetic = 0.5 * jnp.sum(fields[1:4] * velocity, axis=0)
    pressure = (HEAT_RATIO - 1.0) * (fields[4] - kinetic)
    sound_speed = jnp.sqrt(HEAT_RATIO * pressure / fields[0])
    return (velocity, pressure, sound_speed)


def directed(fields, velocity, pressure, sound_speed, direction):
    normal = velocity[direction]
    components = [fields[1 + direction]]
    for component in range(3):
        moment_flux = fields[1 + component] * normal
        if component == direction:
            moment_flux = moment_flux + pressure
        components.append(moment_flux)
    components.append((fields[4] + pressure) * normal)
    return (jnp.stack(components), jnp.abs(normal) + sound_speed)


def tendency(fields):
    velocity, pressure, sound_speed = primitive(fields)
    summed = None
    for direction in range(3):
        fluxes, wave_speed = directed(fields, velocity, pressure, sound_speed, direction)
        if direction < 2:
            dimension = 1 + direction
            extent = fields.shape[dimension]
            left_flux = cut(fluxes, dimension, 0, extent - 1)
            right_flux = cut(fluxes, dimension, 1, extent)
            left_fields = cut(fields, dimension, 0, extent - 1)
            right_fields = cut(fields, dimension, 1, extent)
            bound_speed = jnp.maximum(
                cut(wave_speed, dimension - 1, 0, extent - 1),
                cut(wave_speed, dimension - 1, 1, extent),
            )
        else:
            left_flux = fluxes
            right_flux = jnp.roll(fluxes, -1, axis=3)
            left_fields = fields
            right_fields = jnp.roll(fields, -1, axis=3)
            bound_speed = jnp.maximum(wave_speed, jnp.roll(wave_speed, -1, axis=2))
        face_flux = 0.5 * (left_flux + right_flux) - 0.5 * bound_speed * (
            right_fields - left_fields
        )
        if direction < 2:
            change = cut(face_flux, dimension, 1, extent - 1) - cut(
                face_flux, dimension, 0, extent - 2
            )
            cross_dim = 2 - direction
            change = cut(change, cross_dim, 1, change.shape[cross_dim] - 1)
        else:
            change = face_flux - jnp.roll(face_flux, 1, axis=3)
            change = change[:, 1:-1, 1:-1]
        summed = change if summed is None else summed + change
    return -summed


def ghosted(fields):
    return padded(fields, (("gx", 1), ("gy", 2)), 1)


def shards(density, velocity, pressure, start_block, test_vectors):
    fields = conserved(density[0], velocity[0], pressure[0])
    section_one = fields + TIME_STEP * tendency(ghosted(fields))
    second = 0.5 * fields + 0.5 * (section_one + TIME_STEP * tendency(ghosted(section_one)))
    sampled = second[0, ::2, ::2, ::2]
    flattened = sampled.reshape(-1, sampled.shape[2])
    matrix = flattened - jnp.mean(flattened, axis=1, keepdims=True)
    sketch = jnp.dot(matrix, start_block[0], precision=PRECISE)
    folded = lax.psum(jnp.dot(matrix.T, sketch, precision=PRECISE), ("gx", "gy"))
    member_basis = jnp.dot(matrix, folded, precision=PRECISE)
    stacked = lax.all_gather(member_basis, "member", axis=1, tiled=True)
    vectors = test_vectors.reshape(-1, test_vectors.shape[2])
    gram_matrix, cross_terms = lax.psum(
        (
            jnp.dot(stacked.T, stacked, precision=PRECISE),
            jnp.dot(stacked.T, vectors, precision=PRECISE),
        ),
        ("gx", "gy"),
    )
    factor = jnp.linalg.cholesky(gram_matrix)
    halfway = lax.linalg.triangular_solve(factor, cross_terms, left_side=True, lower=True)
    coefficients = lax.linalg.triangular_solve(
        factor, halfway, left_side=True, lower=True, transpose_a=True
    )
    projected = jnp.dot(stacked, coefficients, precision=PRECISE).reshape(test_vectors.shape)
    return (second[None], projected)


def solution(mesh):
    return jax.shard_map(
        shards,
        mesh=mesh,
        in_specs=(
            P("member", "gx", "gy", None),
            P("member", None, "gx", "gy", None),
            P("member", "gx", "gy", None),
            P("member", None, None),
            P("gx", "gy", None),
        ),
        out_specs=(P("member", None, "gx", "gy", None), P("gx", "gy", None)),
        check_vma=False,
    )
```

profile of v0, /device:TPU:1, one launch (start us, length us, event | category | flops | bytes accessed | tf_op | source)
XLA Modules:
  0.0 560.7 jit_solution(3329118583548477129)
XLA Ops:
  0.7 1.1 bitcast_multiply_fusion.1
  1.8 1.0 fusion.45
  2.9 3.0 collective-permute-start
  5.9 0.2 collective-permute-start.1
  6.1 2.1 collective-permute-done
  8.2 2.8 collective-permute-done.1
  11.0 1.3 collective-permute-start.2
  12.3 1.5 collective-permute-start.3
  13.8 1.3 collective-permute-done.2
  16.0 0.2 multiply_dynamic-update-slice_fusion.15
  16.3 0.4 slice.393
  16.7 0.4 slice.397
  17.2 0.2 fusion.16
  17.6 0.4 fusion.3
  18.0 0.2 fusion.57
  18.2 0.9 slice-done
  19.0 0.7 fusion.6
  19.8 0.2 slice.399
  20.0 0.6 fusion.28
  20.6 1.1 collective-permute-start.4
  21.8 2.1 collective-permute-start.5
  23.8 0.9 collective-permute-done.4
  24.7 1.8 collective-permute-done.5
  26.5 1.3 collective-permute-start.6
  27.8 1.7 collective-permute-start.7
  29.6 1.0 collective-permute-done.6
  31.5 0.2 multiply_dynamic-update-slice_fusion.6
  31.9 0.4 slice.431
  32.3 0.4 slice.435
  32.7 0.2 fusion.13
  33.1 0.4 fusion.1
  33.5 0.2 fusion.56
  33.7 0.9 slice-done.1
  34.6 0.8 fusion.10
  35.4 0.2 slice.437
  35.6 0.6 fusion.23
  36.2 0.7 slice.363
  37.4 0.3 fusion.62
  37.7 250.0 %psum.21 = f32[128,16]{1,0:T(8,128)S(1)} all-reduce(f32[128,16]{1,0:T(8,128)S(1)} %fusion.62), channel_id=1, replica_groups=mesh['gx'=16,'gy'=4,'member'=4] {'gx','gy'}, use_global_device_ids=true, to_apply=%region_4.5 | all-reduce | flops 2048 | bytes 16384 | tf_op jit(solution)/shard_map/psum | solution.py:105
  287.7 0.2 fusion.63
  287.9 9.6 %all_gather.3 = f32[32,64]{0,1:T(8,128)S(1)} all-gather(f32[32,16]{0,1:T(8,128)S(1)} %fusion.63), channel_id=1, replica_groups=mesh['gx'=16,'gy'=4,'member'=4] {'member'}, dimensions={1}, use_global_device_ids=true | all-gather | bytes 10240 | tf_op jit(solution)/shard_map/all_gather | solution.py:107
  297.9 249.3 %all-reduce = (f32[64,128]{1,0:T(8,128)S(1)}, f32[64,64]{0,1:T(8,128)S(1)}) all-reduce(f32[64,128]{1,0:T(8,128)S(1)} %fusion.65, f32[64,64]{0,1:T(8,128)S(1)} %fusion.64), channel_id=1, replica_groups=mesh['gx'=16,'gy'=4,'member'=4] {'gx','gy'}, use_global_device_ids=true, to_apply=%region_8.9 | all-reduce | flops 12288 | bytes 98304 | tf_op jit(solution)/shard_map/psum | solution.py:109
  547.3 5.8 %cholesky.16 = f32[64,64]{1,0:T(8,128)S(1)} custom-call(f32[64,64]{1,0:T(8,128)S(1)} %fusion.51), custom_call_target="Cholesky" | custom-call | tf_op jit(solution)/shard_map/jit(cholesky)/cholesky | solution.py:116
  553.2 0.6 compare_reduce_fusion
  553.8 0.7 fusion.46
  554.5 4.9 custom-call.8
  559.4 0.3 fusion.49
  559.8 0.8 fusion.66
  (67 shorter events, 3.7 us)
Async XLA Ops:
  0.6 297.1 %copy-start = (f32[2,16,128]{2,1,0:T(8,128)S(1)}, f32[2,16,128]{2,1,0:T(8,128)}, u32[]{:S(2)}) copy-start(f32[2,16,128]{2,1,0:T(8,128)} %param.9) | copy-start | bytes 49156
  0.6 2.1 copy-start.3
  2.9 5.3 collective-permute-start
  5.9 5.0 collective-permute-start.1
  11.0 4.0 collective-permute-start.2
  12.3 2.7 collective-permute-start.3
  15.2 1.9 copy-start.1
  18.0 1.1 slice-start
  20.6 4.1 collective-permute-start.4
  21.8 4.7 collective-permute-start.5
  26.5 4.0 collective-permute-start.6
  27.8 2.8 collective-permute-start.7
  30.8 1.9 copy-start.2
  33.5 1.1 slice-start.1
  35.6 1.7 copy-start.5
  36.2 524.4 %copy-start.4 = (f32[5,4,32,256]{3,2,1,0:T(8,128)}, f32[5,4,32,256]{3,2,1,0:T(8,128)S(1)}, u32[]{:S(2)}) copy-start(f32[5,4,32,256]{3,2,1,0:T(8,128)S(1)} %fusion.23) | copy-start | bytes 1966084
where the time goes:
time: 564 us; the launch traced here: 561 us
  blocking collectives  509 us (90%)
  other arithmetic  20.6 us (4%)
  starting transfers between devices  12.2 us (2%)
  waiting for transfers between devices  9.8 us (2%)
  local copies, waits for them, and re-layouts  5.75 us (1%)
    psum x1, blocking collectives, shards(): lax.psum(jnp.dot(matrix.T, sketch, precision=PRECISE), ('gx', 'gy'))  250 us
    psum x1, blocking collectives, shards(): lax.psum((jnp.dot(stacked.T, stacked, precision=PRECISE), jnp.dot(stacked...  249 us
  transfers between devices with their start and end apart: 8, of which 6 were waited for; matrix products, arithmetic and copies ran while one was open for 0% of the time, Pallas kernels for 0%

commit v1 on v0

--- a/solution.py
+++ b/solution.py
@@ -1,11 +1,16 @@
+import functools
+
 import jax
 import jax.numpy as jnp
 from jax import lax
+from jax.experimental import pallas as pl
+from jax.experimental.pallas import tpu as pltpu
 from jax.sharding import PartitionSpec as P
 
 HEAT_RATIO = 1.4
 TIME_STEP = 0.08
 PRECISE = lax.Precision.HIGHEST
+MESH = pl.DeviceIdType.MESH
 
 
 def padded(block, sides, width):
@@ -94,37 +99,214 @@
     return padded(fields, (("gx", 1), ("gy", 2)), 1)
 
 
-def shards(density, velocity, pressure, start_block, test_vectors):
+def dot_nt(left, right):
+    return lax.dot_general(
+        left, right, (((1,), (1,)), ((), ())), precision=PRECISE, preferred_element_type=jnp.float32
+    )
+
+
+def dot_nn(left, right):
+    return lax.dot_general(
+        left, right, (((1,), (0,)), ((), ())), precision=PRECISE, preferred_element_type=jnp.float32
+    )
+
+
+class Place:
+    def __init__(self, nz, ny, nm):
+        self.nz, self.ny, self.nm = nz, ny, nm
+        self.gx = lax.axis_index("gx")
+        self.gy = lax.axis_index("gy")
+        self.m = lax.axis_index("member")
+        self.z = self.gx // 2
+        self.c = self.gx % 2
+        self.plane_index = self.gy * 2 + self.c
+        self.stack_index = self.m * 2 + self.c
+
+    def in_plane(self, step):
+        other = (self.plane_index + step) % (2 * self.ny)
+        return other % 2, (2 * self.z + other % 2, other // 2, self.m)
+
+    def along_z(self, step):
+        return (2 * ((self.z + step) % self.nz) + self.c, self.gy, self.m)
+
+    def in_stack(self, step):
+        other = (self.stack_index + step) % (2 * self.nm)
+        return (2 * self.z + other % 2, self.gy, other // 2)
+
+    def same_cells(self, step):
+        return (self.gx, self.gy, (self.m + step) % self.nm)
+
+    def everyone(self):
+        peers = [self.in_plane(step)[1] for step in range(1, 2 * self.ny)]
+        peers += [self.along_z(step) for step in range(1, self.nz)]
+        peers += [self.in_stack(step) for step in range(1, 2 * self.nm)]
+        return peers
+
+
+def push(src, dst, sems, step, device):
+    copy = pltpu.make_async_remote_copy(
+        src_ref=src,
+        dst_ref=dst,
+        send_sem=sems.at[0, step],
+        recv_sem=sems.at[1, step],
+        device_id=device,
+        device_id_type=MESH,
+    )
+    copy.start()
+    return copy
+
+
+def total(buffer, count):
+    values = [buffer[i] for i in range(count)]
+    while len(values) > 1:
+        pairs = [a + b for a, b in zip(values[::2], values[1::2])]
+        values = pairs + ([values[-1]] if len(values) % 2 else [])
+    return values[0]
+
+
+def reduce_and_gather(place, halves, plane_buf, z_buf, stack_buf, sems):
+    sent = []
+    first = []
+    for step in range(1, 2 * place.ny):
+        core, device = place.in_plane(step)
+        first.append(
+            push(halves.at[core], plane_buf.at[place.plane_index], sems.at[0], step, device)
+        )
+    plane_buf[place.plane_index] = halves[place.c]
+    for copy in first:
+        copy.wait_recv()
+    z_buf[place.z] = total(plane_buf, 2 * place.ny)
+    second = [
+        push(z_buf.at[place.z], z_buf.at[place.z], sems.at[1], step, place.along_z(step))
+        for step in range(1, place.nz)
+    ]
+    for copy in second:
+        copy.wait_recv()
+    stack_buf[place.stack_index] = total(z_buf, place.nz)
+    third = [
+        push(
+            stack_buf.at[place.stack_index],
+            stack_buf.at[place.stack_index],
+            sems.at[2],
+            step,
+            place.in_stack(step),
+        )
+        for step in range(1, 2 * place.nm)
+    ]
+    for copy in third:
+        copy.wait_recv()
+    sent = first + second + third
+    return sent
+
+
+def eliminate(gram, cross):
+    size = gram.shape[0]
+    rows = lax.broadcasted_iota(jnp.int32, (size, 1), 0)
+    scale = jnp.ones((size, 1), jnp.float32)
+    for k in range(size):
+        inverse = 1.0 / gram[k : k + 1, k : k + 1]
+        factor = jnp.where(rows == k, 0.0, gram[:, k : k + 1] * inverse)
+        scale = jnp.where(rows == k, inverse, scale)
+        cross = cross - factor * cross[k : k + 1]
+        gram = gram - factor * gram[k : k + 1]
+    return cross * scale
+
+
+def pod_kernel(
+    nz, ny, nm, sampled, block_t, vectors, out,
+    matrix_all, fold_half, fold_plane, fold_z, fold_all, prod_half, prod_plane, prod_z, prod_all,
+    sems, member_sems,
+):
+    place = Place(nz, ny, nm)
+    rank = block_t.shape[0]
+    barrier = pltpu.get_barrier_semaphore()
+    peers = place.everyone()
+    for device in peers:
+        pl.semaphore_signal(barrier, inc=1, device_id=device, device_id_type=MESH)
+    density = sampled[...]
+    matrix = density - jnp.mean(density, axis=1, keepdims=True)
+    matrix_all[place.m] = matrix
+    fold = dot_nn(dot_nt(block_t[...], matrix), matrix)
+    fold_half[0] = fold[:8]
+    fold_half[1] = fold[8:]
+    pl.semaphore_wait(barrier, len(peers))
+    gathers = [
+        push(
+            matrix_all.at[place.m],
+            matrix_all.at[place.m],
+            member_sems,
+            step,
+            place.same_cells(step),
+        )
+        for step in range(1, nm)
+    ]
+    sent = reduce_and_gather(place, fold_half, fold_plane, fold_z, fold_all, sems.at[0])
+    for copy in gathers:
+        copy.wait_recv()
+    bases_t = [
+        dot_nt(jnp.concatenate([fold_all[2 * i], fold_all[2 * i + 1]], axis=0), matrix_all[i])
+        for i in range(nm)
+    ]
+    stacked_t = jnp.concatenate(bases_t, axis=0)
+    own = jnp.concatenate([fold_all[2 * place.m], fold_all[2 * place.m + 1]], axis=0)
+    own_t = dot_nt(own, matrix)
+    wide = jnp.concatenate(
+        [stacked_t, jnp.zeros((128 - nm * rank, stacked_t.shape[1]), jnp.float32)], axis=0
+    )
+    gram_rows = dot_nt(own_t, wide)
+    cross_rows = dot_nn(own_t, vectors[...])
+    for core in range(2):
+        prod_half[core, :, :128] = gram_rows[8 * core : 8 * core + 8]
+        prod_half[core, :, 128:] = cross_rows[8 * core : 8 * core + 8]
+    sent += reduce_and_gather(place, prod_half, prod_plane, prod_z, prod_all, sems.at[1])
+    both = jnp.concatenate([prod_all[i] for i in range(2 * nm)], axis=0)
+    weights = eliminate(both[:, :128], both[:, 128:])
+    out[...] = dot_nn(stacked_t.T, weights)
+    for copy in sent + gathers:
+        copy.wait_send()
+
+
+def pod(sampled, block_t, vectors, nz, ny, nm):
+    slots = max(2 * ny, nz, 2 * nm)
+    vmem = pl.BlockSpec(memory_space=pltpu.VMEM)
+    f32 = jnp.float32
+    return pl.pallas_call(
+        functools.partial(pod_kernel, nz, ny, nm),
+        out_shape=jax.ShapeDtypeStruct(vectors.shape, f32),
+        in_specs=[vmem] * 3,
+        out_specs=vmem,
+        scratch_shapes=[
+            pltpu.VMEM((nm, *sampled.shape), f32),
+            pltpu.VMEM((2, 8, 128), f32),
+            pltpu.VMEM((2 * ny, 8, 128), f32),
+            pltpu.VMEM((nz, 8, 128), f32),
+            pltpu.VMEM((2 * nm, 8, 128), f32),
+            pltpu.VMEM((2, 8, 256), f32),
+            pltpu.VMEM((2 * ny, 8, 256), f32),
+            pltpu.VMEM((nz, 8, 256), f32),
+            pltpu.VMEM((2 * nm, 8, 256), f32),
+            pltpu.SemaphoreType.DMA((2, 3, 2, slots)),
+            pltpu.SemaphoreType.DMA((2, nm)),
+        ],
+        compiler_params=pltpu.CompilerParams(collective_id=0, has_side_effects=True),
+    )(sampled, block_t, vectors)
+
+
+def shards(sizes, density, velocity, pressure, start_block, test_vectors):
     fields = conserved(density[0], velocity[0], pressure[0])
     section_one = fields + TIME_STEP * tendency(ghosted(fields))
     second = 0.5 * fields + 0.5 * (section_one + TIME_STEP * tendency(ghosted(section_one)))
     sampled = second[0, ::2, ::2, ::2]
     flattened = sampled.reshape(-1, sampled.shape[2])
-    matrix = flattened - jnp.mean(flattened, axis=1, keepdims=True)
-    sketch = jnp.dot(matrix, start_block[0], precision=PRECISE)
-    folded = lax.psum(jnp.dot(matrix.T, sketch, precision=PRECISE), ("gx", "gy"))
-    member_basis = jnp.dot(matrix, folded, precision=PRECISE)
-    stacked = lax.all_gather(member_basis, "member", axis=1, tiled=True)
     vectors = test_vectors.reshape(-1, test_vectors.shape[2])
-    gram_matrix, cross_terms = lax.psum(
-        (
-            jnp.dot(stacked.T, stacked, precision=PRECISE),
-            jnp.dot(stacked.T, vectors, precision=PRECISE),
-        ),
-        ("gx", "gy"),
-    )
-    factor = jnp.linalg.cholesky(gram_matrix)
-    halfway = lax.linalg.triangular_solve(factor, cross_terms, left_side=True, lower=True)
-    coefficients = lax.linalg.triangular_solve(
-        factor, halfway, left_side=True, lower=True, transpose_a=True
-    )
-    projected = jnp.dot(stacked, coefficients, precision=PRECISE).reshape(test_vectors.shape)
+    projected = pod(flattened, start_block[0].T, vectors, *sizes).reshape(test_vectors.shape)
     return (second[None], projected)
 
 
 def solution(mesh):
+    sizes = (mesh.shape["gx"] // 2, mesh.shape["gy"], mesh.shape["member"])
     return jax.shard_map(
-        shards,
+        functools.partial(shards, sizes),
         mesh=mesh,
         in_specs=(
             P("member", "gx", "gy", None),

time: 564 us -> 82.5 us (0.15)
  blocking collectives: 509 us -> 0 us
  Pallas kernels: 0 us -> 43.3 us
  other arithmetic: 20.6 us -> 8.3 us
    psum x2 -> x0, blocking collectives: 499 us -> none  [the longest x1 250 us: shards(): lax.psum(jnp.dot(matrix.T, sketch, precision=PRECISE), ('gx', 'gy'))]
    pallas_call x0 -> x1, Pallas kernels: none -> 43.3 us  [pod(): pl.pallas_call(functools.partial(pod_kernel, nz, ny, nm), out_shape=jax.S...]
    another operation x5 -> x0, other arithmetic: 12.1 us -> none  [the longest x3 6.52 us: shards(): factor = jnp.linalg.cholesky(gram_matrix)]
    all_gather x1 -> x0, blocking collectives: 9.59 us -> none  [shards(): stacked = lax.all_gather(member_basis, 'member', axis=1, tiled=True)]
where the time goes in v1:
time: 82.5 us; the launch traced here: 82.2 us
  Pallas kernels  43.3 us (52%)
  starting transfers between devices  12.2 us (15%)
  waiting for transfers between devices  9.8 us (12%)
  other arithmetic  8.3 us (10%)
  local copies, waits for them, and re-layouts  7.5 us (9%)
  between operations  1.03 us (1%)
    pallas_call x1, Pallas kernels, pod(): pl.pallas_call(functools.partial(pod_kernel, nz, ny, nm), out_shape=jax.S...  43.3 us
    ppermute x4, starting transfers between devices, padded(): lax.ppermute(lax.slice_in_dim(block, block.shape[dim] - width, None, axis...  6.75 us
    ppermute x4, starting transfers between devices, padded(): lax.ppermute(lax.slice_in_dim(block, 0, width, axis=dim), axis, backward)  5.47 us
    ppermute x4, waiting for transfers between devices, padded(): lax.ppermute(lax.slice_in_dim(block, block.shape[dim] - width, None, axis...  5.2 us
    ppermute x4, waiting for transfers between devices, padded(): lax.ppermute(lax.slice_in_dim(block, 0, width, axis=dim), axis, backward)  4.6 us
    sub x6, other arithmetic, tendency(): 0.5 * (left_flux + right_flux)  2.7 us
    slice x6, local copies, waits for them, and re-layouts, tendency(): right_fields = jnp.roll(fields, -1, axis=3)  2.48 us
  transfers between devices with their start and end apart: 8, of which 6 were waited for; matrix products, arithmetic and copies ran while one was open for 0% of the time, Pallas kernels for 0%

profile of v1, /device:TPU:1, one launch (start us, length us, event | category | flops | bytes accessed | tf_op | source)
XLA Modules:
  0.0 82.2 jit_solution(12757271762970298998)
XLA Ops:
  0.6 1.1 %bitcast_multiply_fusion.1 = (f32[3,4,32,256]{3,2,1,0:T(8,128)S(1)}, f32[4,32,256]{2,1,0:T(8,128)S(1)}) fusion(f32[1,3,4,32,256]{4,3,2,1,0:T(8,128)} %param.6, f32[4,32,256]{2,1,0:T(8,128)} %bitcast.79), kind=kLoop, calls=%fused_computation.58 | loop fusion | flops 262144 | bytes 1048576 | tf_op jit(solution)/shard_map/mul | solution.py:35
  1.8 1.0 %fusion.45 = f32[1,4,32,256]{3,2,1,0:T(8,128)S(1)} fusion(f32[4,32,256]{2,1,0:T(8,128)S(1)} %get-tuple-element.63, f32[1,4,32,256]{3,2,1,0:T(8,128)} %param.5, f32[1,4,32,256]{3,2,1,0:T(8,128)} %param.7), kind=kLoop, calls=%fused_computation.127 | loop fusion | flops 131072 | bytes 524288 | tf_op jit(solution)/shard_map/add | solution.py:36
  2.9 3.0 %collective-permute-start = (f32[5,1,32,256]{3,2,1,0:T(8,128)S(1)}, f32[5,1,32,256]{3,2,1,0:T(8,128)S(1)}, u32[]{:S(2)}, u32[]{:S(2)}) collective-permute-start(f32[5,1,32,256]{3,2,1,0:T(8,128)S(1)} %get-tuple-element.60), channel_id=1, source_target_pairs={{0,16},{16,32},{32,48},{48,64},{64,80},{80,96},{96,112},{112,128},... | collective-permute-start | bytes 491528 | tf_op jit(solution)/shard_map/ppermute | solution.py:22
  5.9 0.2 collective-permute-start.1
  6.1 2.1 %collective-permute-done = f32[5,1,32,256]{3,2,1,0:T(8,128)S(1)} collective-permute-done((f32[5,1,32,256]{3,2,1,0:T(8,128)S(1)}, f32[5,1,32,256]{3,2,1,0:T(8,128)S(1)}, u32[]{:S(2)}, u32[]{:S(2)}) %collective-permute-start) | collective-permute-done | bytes 163872 | tf_op jit(solution)/shard_map/ppermute | solution.py:22
  8.2 2.8 %collective-permute-done.1 = f32[5,1,32,256]{3,2,1,0:T(8,128)S(1)} collective-permute-done((f32[5,1,32,256]{3,2,1,0:T(8,128)S(1)}, f32[5,1,32,256]{3,2,1,0:T(8,128)S(1)}, u32[]{:S(2)}, u32[]{:S(2)}) %collective-permute-start.1) | collective-permute-done | bytes 163872 | tf_op jit(solution)/shard_map/ppermute | solution.py:25
  11.0 1.3 %collective-permute-start.2 = (f32[5,6,1,256]{3,2,1,0:T(1,128)S(1)}, f32[5,6,1,256]{3,2,1,0:T(1,128)S(1)}, u32[]{:S(2)}, u32[]{:S(2)}) collective-permute-start(f32[5,6,1,256]{3,2,1,0:T(1,128)S(1)} %get-tuple-element.56), channel_id=1, source_target_pairs={{0,4},{4,8},{8,12},{12,0},{1,5},{5,9},{9,13},{13,1},{2,6},{6,10},{... | collective-permute-start | bytes 92168 | tf_op jit(solution)/shard_map/ppermute | solution.py:22
  12.3 1.5 %collective-permute-start.3 = (f32[5,6,1,256]{3,2,1,0:T(1,128)S(1)}, f32[5,6,1,256]{3,2,1,0:T(1,128)S(1)}, u32[]{:S(2)}, u32[]{:S(2)}) collective-permute-start(f32[5,6,1,256]{3,2,1,0:T(1,128)S(1)} %get-tuple-element.57), channel_id=1, source_target_pairs={{4,0},{8,4},{12,8},{0,12},{5,1},{9,5},{13,9},{1,13},{6,2},{10,6},{... | collective-permute-start | bytes 92168 | tf_op jit(solution)/shard_map/ppermute | solution.py:25
  13.7 1.3 %collective-permute-done.2 = f32[5,6,1,256]{3,2,1,0:T(1,128)S(1)} collective-permute-done((f32[5,6,1,256]{3,2,1,0:T(1,128)S(1)}, f32[5,6,1,256]{3,2,1,0:T(1,128)S(1)}, u32[]{:S(2)}, u32[]{:S(2)}) %collective-permute-start.2) | collective-permute-done | bytes 30752 | tf_op jit(solution)/shard_map/ppermute | solution.py:22
  15.0 0.2 pad_maximum_fusion
  15.2 0.1 multiply_reduce_fusion.1
  15.3 0.1 bitcast_add_fusion.5
  15.5 0.1 slice_bitcast_fusion.1
  16.0 0.2 multiply_dynamic-update-slice_fusion.15
  16.3 0.4 slice.379
  16.7 0.4 slice.383
  17.1 0.2 fusion.16
  17.3 0.1 fusion.51
  17.5 0.4 fusion.3
  18.0 0.2 fusion.49
  18.2 0.9 %slice-done = f32[5,6,34,1]{3,2,1,0:T(8,128)S(1)} async-done(((f32[5,6,34,256]{3,2,1,0:T(8,128)}), f32[5,6,34,1]{3,2,1,0:T(8,128)S(1)}, s32[]{:S(2)}) %slice-start) | async-done | bytes 4104 | tf_op jit(solution)/shard_map/jit(_roll_static)/slice | solution.py:80
  19.0 0.7 fusion.6
  19.8 0.2 slice.385
  20.0 0.6 fusion.28
  20.6 1.1 %collective-permute-start.4 = (f32[5,1,32,256]{3,2,1,0:T(8,128)S(1)}, f32[5,1,32,256]{3,2,1,0:T(8,128)S(1)}, u32[]{:S(2)}, u32[]{:S(2)}) collective-permute-start(f32[5,1,32,256]{3,2,1,0:T(8,128)S(1)} %get-tuple-element.58), channel_id=1, source_target_pairs={{0,16},{16,32},{32,48},{48,64},{64,80},{80,96},{96,112},{112,128},... | collective-permute-start | bytes 491528 | tf_op jit(solution)/shard_map/ppermute | solution.py:22
  21.7 2.1 %collective-permute-start.5 = (f32[5,1,32,256]{3,2,1,0:T(8,128)S(1)}, f32[5,1,32,256]{3,2,1,0:T(8,128)S(1)}, u32[]{:S(2)}, u32[]{:S(2)}) collective-permute-start(f32[5,1,32,256]{3,2,1,0:T(8,128)S(1)} %get-tuple-element.59), channel_id=1, source_target_pairs={{16,0},{32,16},{48,32},{64,48},{80,64},{96,80},{112,96},{128,112},... | collective-permute-start | bytes 491528 | tf_op jit(solution)/shard_map/ppermute | solution.py:25
  23.8 0.9 %collective-permute-done.4 = f32[5,1,32,256]{3,2,1,0:T(8,128)S(1)} collective-permute-done((f32[5,1,32,256]{3,2,1,0:T(8,128)S(1)}, f32[5,1,32,256]{3,2,1,0:T(8,128)S(1)}, u32[]{:S(2)}, u32[]{:S(2)}) %collective-permute-start.4) | collective-permute-done | bytes 163872 | tf_op jit(solution)/shard_map/ppermute | solution.py:22
  24.7 1.8 %collective-permute-done.5 = f32[5,1,32,256]{3,2,1,0:T(8,128)S(1)} collective-permute-done((f32[5,1,32,256]{3,2,1,0:T(8,128)S(1)}, f32[5,1,32,256]{3,2,1,0:T(8,128)S(1)}, u32[]{:S(2)}, u32[]{:S(2)}) %collective-permute-start.5) | collective-permute-done | bytes 163872 | tf_op jit(solution)/shard_map/ppermute | solution.py:25
  26.5 1.3 %collective-permute-start.6 = (f32[5,6,1,256]{3,2,1,0:T(1,128)S(1)}, f32[5,6,1,256]{3,2,1,0:T(1,128)S(1)}, u32[]{:S(2)}, u32[]{:S(2)}) collective-permute-start(f32[5,6,1,256]{3,2,1,0:T(1,128)S(1)} %get-tuple-element.52), channel_id=1, source_target_pairs={{0,4},{4,8},{8,12},{12,0},{1,5},{5,9},{9,13},{13,1},{2,6},{6,10},{... | collective-permute-start | bytes 92168 | tf_op jit(solution)/shard_map/ppermute | solution.py:22
  27.8 1.7 %collective-permute-start.7 = (f32[5,6,1,256]{3,2,1,0:T(1,128)S(1)}, f32[5,6,1,256]{3,2,1,0:T(1,128)S(1)}, u32[]{:S(2)}, u32[]{:S(2)}) collective-permute-start(f32[5,6,1,256]{3,2,1,0:T(1,128)S(1)} %get-tuple-element.53), channel_id=1, source_target_pairs={{4,0},{8,4},{12,8},{0,12},{5,1},{9,5},{13,9},{1,13},{6,2},{10,6},{... | collective-permute-start | bytes 92168 | tf_op jit(solution)/shard_map/ppermute | solution.py:25
  29.6 1.0 %collective-permute-done.6 = f32[5,6,1,256]{3,2,1,0:T(1,128)S(1)} collective-permute-done((f32[5,6,1,256]{3,2,1,0:T(1,128)S(1)}, f32[5,6,1,256]{3,2,1,0:T(1,128)S(1)}, u32[]{:S(2)}, u32[]{:S(2)}) %collective-permute-start.6) | collective-permute-done | bytes 30752 | tf_op jit(solution)/shard_map/ppermute | solution.py:22
  30.6 0.2 pad_maximum_fusion.1
  30.9 0.1 bitcast_add_fusion.2
  31.1 0.1 slice_bitcast_fusion
  31.5 0.2 multiply_dynamic-update-slice_fusion.6
  31.9 0.4 slice.417
  32.3 0.4 slice.421
  32.7 0.2 fusion.13
  32.9 0.1 fusion.50
  33.1 0.4 fusion.1
  33.5 0.2 fusion.48
  33.7 0.9 %slice-done.1 = f32[5,6,34,1]{3,2,1,0:T(8,128)S(1)} async-done(((f32[5,6,34,256]{3,2,1,0:T(8,128)}), f32[5,6,34,1]{3,2,1,0:T(8,128)S(1)}, s32[]{:S(2)}) %slice-start.1) | async-done | bytes 4104 | tf_op jit(solution)/shard_map/jit(_roll_static)/slice | solution.py:80
  34.6 0.8 fusion.10
  35.3 0.2 slice.423
  35.6 0.6 fusion.23
  36.2 1.3 %slice.349 = f32[1,2,16,128]{3,2,1,0:T(8,128)} slice(f32[5,4,32,256]{3,2,1,0:T(8,128)S(1)} %fusion.23), slice={[0:1:1], [0:4:2], [0:32:2], [0:256:2]} | slice | bytes 32768 | tf_op jit(solution)/shard_map/slice | solution.py:299
  37.5 43.3 %shard_map.68 = f32[32,128]{1,0:T(8,128)} custom-call(f32[32,128]{1,0:T(8,128)} %bitcast.82, f32[16,128]{1,0:T(8,128)} %bitcast.84, f32[32,128]{1,0:T(8,128)} %bitcast.83), custom_call_target="tpu_custom_call" | custom-call | tf_op jit(solution)/shard_map/pallas_call | solution.py:273
  80.9 1.3 %copy.86 = f32[2,16,128]{2,1,0:T(8,128)} copy(f32[2,16,128]{2,1,0:T(8,128)} %bitcast.81) | data formatting | bytes 32768
  (42 shorter events, 1.4 us)
Async XLA Ops:
  0.6 2.1 %copy-start.2 = (f32[1,4,32,256]{3,2,1,0:T(8,128)S(1)}, f32[1,4,32,256]{3,2,1,0:T(8,128)}, u32[]{:S(2)}) copy-start(f32[1,4,32,256]{3,2,1,0:T(8,128)} %param.5) | copy-start | bytes 393220
  2.9 5.3 %collective-permute-start = (f32[5,1,32,256]{3,2,1,0:T(8,128)S(1)}, f32[5,1,32,256]{3,2,1,0:T(8,128)S(1)}, u32[]{:S(2)}, u32[]{:S(2)}) collective-permute-start(f32[5,1,32,256]{3,2,1,0:T(8,128)S(1)} %get-tuple-element.60), channel_id=1, source_target_pairs={{0,16},{16,32},{32,48},{48,64},{64,80},{80,96},{96,112},{112,128},... | collective-permute-start | bytes 491528 | tf_op jit(solution)/shard_map/ppermute | solution.py:22
  5.9 5.0 %collective-permute-start.1 = (f32[5,1,32,256]{3,2,1,0:T(8,128)S(1)}, f32[5,1,32,256]{3,2,1,0:T(8,128)S(1)}, u32[]{:S(2)}, u32[]{:S(2)}) collective-permute-start(f32[5,1,32,256]{3,2,1,0:T(8,128)S(1)} %get-tuple-element.61), channel_id=1, source_target_pairs={{16,0},{32,16},{48,32},{64,48},{80,64},{96,80},{112,96},{128,112},... | collective-permute-start | bytes 491528 | tf_op jit(solution)/shard_map/ppermute | solution.py:25
  11.0 4.0 %collective-permute-start.2 = (f32[5,6,1,256]{3,2,1,0:T(1,128)S(1)}, f32[5,6,1,256]{3,2,1,0:T(1,128)S(1)}, u32[]{:S(2)}, u32[]{:S(2)}) collective-permute-start(f32[5,6,1,256]{3,2,1,0:T(1,128)S(1)} %get-tuple-element.56), channel_id=1, source_target_pairs={{0,4},{4,8},{8,12},{12,0},{1,5},{5,9},{9,13},{13,1},{2,6},{6,10},{... | collective-permute-start | bytes 92168 | tf_op jit(solution)/shard_map/ppermute | solution.py:22
  12.3 2.7 %collective-permute-start.3 = (f32[5,6,1,256]{3,2,1,0:T(1,128)S(1)}, f32[5,6,1,256]{3,2,1,0:T(1,128)S(1)}, u32[]{:S(2)}, u32[]{:S(2)}) collective-permute-start(f32[5,6,1,256]{3,2,1,0:T(1,128)S(1)} %get-tuple-element.57), channel_id=1, source_target_pairs={{4,0},{8,4},{12,8},{0,12},{5,1},{9,5},{13,9},{1,13},{6,2},{10,6},{... | collective-permute-start | bytes 92168 | tf_op jit(solution)/shard_map/ppermute | solution.py:25
  15.2 1.9 %copy-start = (f32[5,6,34,256]{3,2,1,0:T(8,128)}, f32[5,6,34,256]{3,2,1,0:T(8,128)S(1)}, u32[]{:S(2)}) copy-start(f32[5,6,34,256]{3,2,1,0:T(8,128)S(1)} %pad_maximum_fusion) | copy-start | bytes 3133444
  18.0 1.1 %slice-start = ((f32[5,6,34,256]{3,2,1,0:T(8,128)}), f32[5,6,34,1]{3,2,1,0:T(8,128)S(1)}, s32[]{:S(2)}) async-start(f32[5,6,34,256]{3,2,1,0:T(8,128)} %copy-done), calls=%async_computation | async-start | bytes 1228800 | tf_op jit(solution)/shard_map/jit(_roll_static)/slice | solution.py:80
  20.6 4.1 %collective-permute-start.4 = (f32[5,1,32,256]{3,2,1,0:T(8,128)S(1)}, f32[5,1,32,256]{3,2,1,0:T(8,128)S(1)}, u32[]{:S(2)}, u32[]{:S(2)}) collective-permute-start(f32[5,1,32,256]{3,2,1,0:T(8,128)S(1)} %get-tuple-element.58), channel_id=1, source_target_pairs={{0,16},{16,32},{32,48},{48,64},{64,80},{80,96},{96,112},{112,128},... | collective-permute-start | bytes 491528 | tf_op jit(solution)/shard_map/ppermute | solution.py:22
  21.7 4.7 %collective-permute-start.5 = (f32[5,1,32,256]{3,2,1,0:T(8,128)S(1)}, f32[5,1,32,256]{3,2,1,0:T(8,128)S(1)}, u32[]{:S(2)}, u32[]{:S(2)}) collective-permute-start(f32[5,1,32,256]{3,2,1,0:T(8,128)S(1)} %get-tuple-element.59), channel_id=1, source_target_pairs={{16,0},{32,16},{48,32},{64,48},{80,64},{96,80},{112,96},{128,112},... | collective-permute-start | bytes 491528 | tf_op jit(solution)/shard_map/ppermute | solution.py:25
  26.5 4.0 %collective-permute-start.6 = (f32[5,6,1,256]{3,2,1,0:T(1,128)S(1)}, f32[5,6,1,256]{3,2,1,0:T(1,128)S(1)}, u32[]{:S(2)}, u32[]{:S(2)}) collective-permute-start(f32[5,6,1,256]{3,2,1,0:T(1,128)S(1)} %get-tuple-element.52), channel_id=1, source_target_pairs={{0,4},{4,8},{8,12},{12,0},{1,5},{5,9},{9,13},{13,1},{2,6},{6,10},{... | collective-permute-start | bytes 92168 | tf_op jit(solution)/shard_map/ppermute | solution.py:22
  27.8 2.8 %collective-permute-start.7 = (f32[5,6,1,256]{3,2,1,0:T(1,128)S(1)}, f32[5,6,1,256]{3,2,1,0:T(1,128)S(1)}, u32[]{:S(2)}, u32[]{:S(2)}) collective-permute-start(f32[5,6,1,256]{3,2,1,0:T(1,128)S(1)} %get-tuple-element.53), channel_id=1, source_target_pairs={{4,0},{8,4},{12,8},{0,12},{5,1},{9,5},{13,9},{1,13},{6,2},{10,6},{... | collective-permute-start | bytes 92168 | tf_op jit(solution)/shard_map/ppermute | solution.py:25
  30.7 1.9 %copy-start.1 = (f32[5,6,34,256]{3,2,1,0:T(8,128)}, f32[5,6,34,256]{3,2,1,0:T(8,128)S(1)}, u32[]{:S(2)}) copy-start(f32[5,6,34,256]{3,2,1,0:T(8,128)S(1)} %pad_maximum_fusion.1) | copy-start | bytes 3133444
  33.5 1.1 %slice-start.1 = ((f32[5,6,34,256]{3,2,1,0:T(8,128)}), f32[5,6,34,1]{3,2,1,0:T(8,128)S(1)}, s32[]{:S(2)}) async-start(f32[5,6,34,256]{3,2,1,0:T(8,128)} %copy-done.1), calls=%async_computation.1 | async-start | bytes 1228800 | tf_op jit(solution)/shard_map/jit(_roll_static)/slice | solution.py:80
  36.2 46.0 %copy-start.3 = (f32[5,4,32,256]{3,2,1,0:T(8,128)}, f32[5,4,32,256]{3,2,1,0:T(8,128)S(1)}, u32[]{:S(2)}) copy-start(f32[5,4,32,256]{3,2,1,0:T(8,128)S(1)} %fusion.23) | copy-start | bytes 1966084

commit v2 on v1

v2 whole, which is shorter than its diff:
```python
import functools

import jax
import jax.numpy as jnp
from jax import lax
from jax.experimental import pallas as pl
from jax.experimental.pallas import tpu as pltpu
from jax.sharding import PartitionSpec as P

HEAT_RATIO = 1.4
TIME_STEP = 0.08
HALF_STEP = 0.5 * TIME_STEP
PRECISE = lax.Precision.HIGHEST
MESH = pl.DeviceIdType.MESH

PLANES, ROWS, OWN_ROWS = 8, 40, 32
RHO, VEL, PRES, MOM, ENERGY, SOUND = 0, 1, 4, 5, 8, 9
CONSERVED = (RHO, MOM, MOM + 1, MOM + 2, ENERGY)


def dot_nt(left, right):
    return lax.dot_general(
        left, right, (((1,), (1,)), ((), ())), precision=PRECISE, preferred_element_type=jnp.float32
    )


def dot_nn(left, right):
    return lax.dot_general(
        left, right, (((1,), (0,)), ((), ())), precision=PRECISE, preferred_element_type=jnp.float32
    )


class Place:
    def __init__(self, nz, ny, nm):
        self.nz, self.ny, self.nm = nz, ny, nm
        self.gx = lax.axis_index("gx")
        self.gy = lax.axis_index("gy")
        self.m = lax.axis_index("member")
        self.z = self.gx // 2
        self.c = self.gx % 2
        self.plane_index = self.gy * 2 + self.c
        self.stack_index = self.m * 2 + self.c

    def neighbour(self, up_x, up_y):
        nx = 2 * self.nz
        return ((self.gx + up_x + nx) % nx, (self.gy + up_y + self.ny) % self.ny, self.m)

    def in_plane(self, step):
        other = (self.plane_index + step) % (2 * self.ny)
        return other % 2, (2 * self.z + other % 2, other // 2, self.m)

    def along_z(self, step):
        return (2 * ((self.z + step) % self.nz) + self.c, self.gy, self.m)

    def in_stack(self, step):
        other = (self.stack_index + step) % (2 * self.nm)
        return (2 * self.z + other % 2, self.gy, other // 2)

    def same_cells(self, step):
        return (self.gx, self.gy, (self.m + step) % self.nm)

    def everyone(self):
        peers = [self.neighbour(x, y) for x in (-1, 0, 1) for y in (-1, 0, 1) if (x, y) != (0, 0)]
        peers += [self.in_plane(step)[1] for step in range(1, 2 * self.ny)]
        peers += [self.along_z(step) for step in range(1, self.nz)]
        peers += [self.in_stack(step) for step in range(1, 2 * self.nm)]
        return peers


def push(src, dst, send_sem, recv_sem, device):
    copy = pltpu.make_async_remote_copy(
        src_ref=src,
        dst_ref=dst,
        send_sem=send_sem,
        recv_sem=recv_sem,
        device_id=device,
        device_id_type=MESH,
    )
    copy.start()
    return copy


def total(buffer, count):
    values = [buffer[i] for i in range(count)]
    while len(values) > 1:
        pairs = [a + b for a, b in zip(values[::2], values[1::2])]
        values = pairs + ([values[-1]] if len(values) % 2 else [])
    return values[0]


def reduce_and_gather(place, halves, plane_buf, z_buf, stack_buf, sems, meanwhile):
    first = []
    for step in range(1, 2 * place.ny):
        core, device = place.in_plane(step)
        first.append(
            push(
                halves.at[core],
                plane_buf.at[place.plane_index],
                sems.at[0, 0, step],
                sems.at[0, 1, step],
                device,
            )
        )
    plane_buf[place.plane_index] = halves[place.c]
    meanwhile[0]()
    for copy in first:
        copy.wait_recv()
    z_buf[place.z] = total(plane_buf, 2 * place.ny)
    second = [
        push(
            z_buf.at[place.z],
            z_buf.at[place.z],
            sems.at[1, 0, step],
            sems.at[1, 1, step],
            place.along_z(step),
        )
        for step in range(1, place.nz)
    ]
    meanwhile[1]()
    for copy in second:
        copy.wait_recv()
    stack_buf[place.stack_index] = total(z_buf, place.nz)
    third = [
        push(
            stack_buf.at[place.stack_index],
            stack_buf.at[place.stack_index],
            sems.at[2, 0, step],
            sems.at[2, 1, step],
            place.in_stack(step),
        )
        for step in range(1, 2 * place.nm)
    ]
    meanwhile[2]()
    for copy in third:
        copy.wait_recv()
    return first + second + third


def eliminate(gram, cross):
    size = gram.shape[0]
    rows = lax.broadcasted_iota(jnp.int32, (size, 1), 0)
    scale = jnp.ones((size, 1), jnp.float32)
    for k in range(size):
        inverse = 1.0 / gram[k : k + 1, k : k + 1]
        factor = jnp.where(rows == k, 0.0, gram[:, k : k + 1] * inverse)
        scale = jnp.where(rows == k, inverse, scale)
        cross = cross - factor * cross[k : k + 1]
        gram = gram - factor * gram[k : k + 1]
    return cross * scale


def ahead(values, axis):
    return pltpu.roll(values, values.shape[axis] - 1, axis)


def behind(values, axis):
    return pltpu.roll(values, 1, axis)


def flux(cells, plane, field, direction, pressure, normal):
    value = cells[field, plane]
    if field == RHO:
        return cells[MOM + direction, plane], value
    if field == ENERGY:
        return (value + pressure) * normal, value
    result = value * normal
    return (result + pressure if field == MOM + direction else result), value


def first_faces(cells, faces, plane, fields):
    low_v, high_v = cells[VEL, plane], cells[VEL, plane + 1]
    low_p, high_p = cells[PRES, plane], cells[PRES, plane + 1]
    speed = jnp.maximum(
        jnp.abs(low_v) + cells[SOUND, plane], jnp.abs(high_v) + cells[SOUND, plane + 1]
    )
    for field in fields:
        low_f, low_u = flux(cells, plane, field, 0, low_p, low_v)
        high_f, high_u = flux(cells, plane + 1, field, 0, high_p, high_v)
        faces[CONSERVED.index(field), plane] = (low_f + high_f) - speed * (high_u - low_u)


def changes(cells, faces, plane, fields):
    sums = [faces[CONSERVED.index(f), plane] - faces[CONSERVED.index(f), plane - 1] for f in fields]
    pressure, sound = cells[PRES, plane], cells[SOUND, plane]
    for direction in (1, 2):
        axis = direction - 1
        normal = cells[VEL + direction, plane]
        speed = jnp.abs(normal) + sound
        speed = jnp.maximum(speed, ahead(speed, axis))
        for at, field in enumerate(fields):
            here, value = flux(cells, plane, field, direction, pressure, normal)
            face = (here + ahead(here, axis)) - speed * (ahead(value, axis) - value)
            sums[at] = sums[at] + (face - behind(face, axis))
    return sums


def complete_initial(cells, plane, rows):
    rho, pressure = cells[RHO, plane, rows], cells[PRES, plane, rows]
    squares = None
    for k in range(3):
        velocity = cells[VEL + k, plane, rows]
        cells[MOM + k, plane, rows] = rho * velocity
        squares = velocity * velocity if squares is None else squares + velocity * velocity
    cells[ENERGY, plane, rows] = pressure * (1.0 / (HEAT_RATIO - 1.0)) + 0.5 * rho * squares
    cells[SOUND, plane, rows] = jnp.sqrt(HEAT_RATIO * pressure / rho)


def first_stage(cells, faces, after, plane):
    sums = changes(cells, faces, plane, CONSERVED)
    values = [cells[f, plane] - HALF_STEP * s for f, s in zip(CONSERVED, sums)]
    rho, energy = values[0], values[4]
    inverse = 1.0 / rho
    kinetic = None
    for k in range(3):
        velocity = values[1 + k] * inverse
        after[MOM + k, plane] = values[1 + k]
        after[VEL + k, plane] = velocity
        term = values[1 + k] * velocity
        kinetic = term if kinetic is None else kinetic + term
    pressure = (HEAT_RATIO - 1.0) * (energy - 0.5 * kinetic)
    after[RHO, plane] = rho
    after[ENERGY, plane] = energy
    after[PRES, plane] = pressure
    after[SOUND, plane] = jnp.sqrt(HEAT_RATIO * pressure * inverse)


def second_stage(cells, after, faces, result, plane, fields):
    sums = changes(after, faces, plane, fields)
    for field, s in zip(fields, sums):
        value = 0.5 * cells[field, plane] + 0.5 * (after[field, plane] - HALF_STEP * s)
        result[CONSERVED.index(field), plane - 2] = value[:OWN_ROWS]


def over(first, stop, body):
    lax.fori_loop(first, stop, lambda i, carry: (body(i), carry)[1], 0)


def window_kernel(
    nz, ny, nm, density, velocity, pressure, block, test, state, out,
    cells, after, faces, result, row_send, row_recv, corner_send, corner_recv, pick, thin,
    block_in, test_in,
    matrix_all, fold_half, fold_plane, fold_z, fold_all, prod_half, prod_plane, prod_z, prod_all,
    local_sems, halo_sems, sems, member_sems,
):
    place = Place(nz, ny, nm)
    rank = block.shape[2]
    snaps = block.shape[1]
    barrier = pltpu.get_barrier_semaphore()
    peers = place.everyone()
    own = pl.ds(0, OWN_ROWS)
    loads = [
        pltpu.make_async_copy(density.at[0], cells.at[RHO, 2:6, own], local_sems.at[0]),
        pltpu.make_async_copy(velocity.at[0], cells.at[VEL : VEL + 3, 2:6, own], local_sems.at[1]),
        pltpu.make_async_copy(pressure.at[0], cells.at[PRES, 2:6, own], local_sems.at[2]),
    ]
    late_loads = [
        pltpu.make_async_copy(block.at[0], block_in, local_sems.at[3]),
        pltpu.make_async_copy(test, test_in, local_sems.at[4]),
    ]
    for copy in loads + late_loads:
        copy.start()
    for device in peers:
        pl.semaphore_signal(barrier, inc=1, device_id=device, device_id_type=MESH)
    row = lax.broadcasted_iota(jnp.int32, pick.shape, 0)
    column = lax.broadcasted_iota(jnp.int32, pick.shape, 1)
    pick[...] = jnp.where(row == 2 * column, 1.0, 0.0) - jnp.where(row % 2 == 0, 1.0 / snaps, 0.0)
    for copy in loads:
        copy.wait()
    raw = slice(0, 5)
    for i in range(4):
        row_send[0, :, 2 * i : 2 * i + 2] = cells[raw, 2 + i, OWN_ROWS - 2 : OWN_ROWS]
        row_send[1, :, 2 * i : 2 * i + 2] = cells[raw, 2 + i, 0:2]
    corners = ((1, 1), (1, -1), (-1, 1), (-1, -1))
    for at, (up_x, up_y) in enumerate(corners):
        line = OWN_ROWS - 1 if up_y == 1 else 0
        for f in range(5):
            corner_send[at, f : f + 1] = cells[f, 5 if up_x == 1 else 2, line : line + 1]
    pl.semaphore_wait(barrier, len(peers))

    def plane_push(index, source, target, up_x):
        return push(
            cells.at[raw, source, own],
            cells.at[raw, target, own],
            halo_sems.at[0, index],
            halo_sems.at[1, index],
            place.neighbour(up_x, 0),
        )

    up_near, down_near = plane_push(0, 5, 1, 1), plane_push(1, 2, 6, -1)
    row_copies = [
        push(
            row_send.at[i],
            row_recv.at[i],
            halo_sems.at[0, 2 + i],
            halo_sems.at[1, 2 + i],
            place.neighbour(0, 1 - 2 * i),
        )
        for i in range(2)
    ]
    corner_copies = [
        push(
            corner_send.at[i],
            corner_recv.at[i],
            halo_sems.at[0, 4 + i],
            halo_sems.at[1, 4 + i],
            place.neighbour(*corners[i]),
        )
        for i in range(4)
    ]
    up_far, down_far = plane_push(8, 4, 0, 1), plane_push(9, 3, 7, -1)
    sent = [up_near, down_near, *row_copies, *corner_copies, up_far, down_far]

    over(2, 6, lambda p: complete_initial(cells, p, own))
    halo = pl.ds(OWN_ROWS, ROWS - OWN_ROWS)
    for copy in row_copies:
        copy.wait_recv()
    for i in range(4):
        cells[raw, 2 + i, ROWS - 2 : ROWS] = row_recv[0, :, 2 * i : 2 * i + 2]
        cells[raw, 2 + i, OWN_ROWS : OWN_ROWS + 2] = row_recv[1, :, 2 * i : 2 * i + 2]
    over(2, 6, lambda p: complete_initial(cells, p, halo))
    over(2, 5, lambda p: first_faces(cells, faces, p, CONSERVED))
    over(3, 5, lambda p: first_stage(cells, faces, after, p))

    for copy in corner_copies:
        copy.wait_recv()
    for at, (up_x, up_y) in enumerate(corners):
        line = ROWS - 1 if up_y == 1 else OWN_ROWS
        for f in range(5):
            cells[f, 1 if up_x == 1 else 6, line : line + 1] = corner_recv[at, f : f + 1]
    everything = pl.ds(0, ROWS)
    for copy, near, face, inner in ((down_near, 6, 5, 5), (up_near, 1, 1, 2)):
        copy.wait_recv()
        complete_initial(cells, near, everything)
        first_faces(cells, faces, face, CONSERVED)
        first_stage(cells, faces, after, inner)
    mass = (RHO,)
    rest = CONSERVED[1:]
    over(2, 5, lambda p: first_faces(after, faces, p, mass))
    second_stage(cells, after, faces, result, 4, mass)
    up_far.wait_recv()
    complete_initial(cells, 0, everything)
    first_faces(cells, faces, 0, CONSERVED)
    first_stage(cells, faces, after, 1)
    first_faces(after, faces, 1, mass)
    second_stage(cells, after, faces, result, 2, mass)

    even = pl.ds(0, OWN_ROWS // 2, stride=2)
    for i in range(2):
        for side in range(2):
            lanes = slice(128 * side, 128 * side + 128)
            thin[2 * i + side] = result[0, 2 * i, :, lanes]
    sampled = jnp.concatenate(
        [jnp.concatenate([thin[2 * i, even], thin[2 * i + 1, even]], axis=1) for i in range(2)],
        axis=0,
    )
    matrix = dot_nn(sampled, pick[...])
    matrix_all[place.m] = matrix
    for copy in late_loads:
        copy.wait()
    fold = dot_nn(dot_nt(block_in[...].T, matrix), matrix)
    fold_half[0] = fold[:8]
    fold_half[1] = fold[8:]
    gathers = [
        push(
            matrix_all.at[place.m],
            matrix_all.at[place.m],
            member_sems.at[0, step],
            member_sems.at[1, step],
            place.same_cells(step),
        )
        for step in range(1, nm)
    ]

    def last_plane():
        down_far.wait_recv()
        complete_initial(cells, 7, everything)
        first_faces(cells, faces, 6, CONSERVED)
        first_stage(cells, faces, after, 6)

    def other_fields():
        first_faces(after, faces, 5, mass)
        second_stage(cells, after, faces, result, 3, mass)
        second_stage(cells, after, faces, result, 5, mass)
        over(1, 6, lambda p: first_faces(after, faces, p, rest))
        over(2, 6, lambda p: second_stage(cells, after, faces, result, p, rest))

    store = pltpu.make_async_copy(result, state.at[0], local_sems.at[5])

    def nothing():
        pass

    sent += reduce_and_gather(
        place, fold_half, fold_plane, fold_z, fold_all, sems.at[0],
        (last_plane, other_fields, store.start),
    )
    for copy in gathers:
        copy.wait_recv()
    bases_t = [
        dot_nt(jnp.concatenate([fold_all[2 * i], fold_all[2 * i + 1]], axis=0), matrix_all[i])
        for i in range(nm)
    ]
    stacked_t = jnp.concatenate(bases_t, axis=0)
    own_fold = jnp.concatenate([fold_all[2 * place.m], fold_all[2 * place.m + 1]], axis=0)
    own_t = dot_nt(own_fold, matrix)
    wide = jnp.concatenate(
        [stacked_t, jnp.zeros((128 - nm * rank, stacked_t.shape[1]), jnp.float32)], axis=0
    )
    gram_rows = dot_nt(own_t, wide)
    vectors = jnp.concatenate([test_in[0], test_in[1]], axis=0)
    cross_rows = dot_nn(own_t, vectors)
    for core in range(2):
        prod_half[core, :, :128] = gram_rows[8 * core : 8 * core + 8]
        prod_half[core, :, 128:] = cross_rows[8 * core : 8 * core + 8]
    sent += reduce_and_gather(
        place, prod_half, prod_plane, prod_z, prod_all, sems.at[1], (nothing, nothing, nothing)
    )
    both = jnp.concatenate([prod_all[i] for i in range(2 * nm)], axis=0)
    weights = eliminate(both[:, :128], both[:, 128:])
    projected = dot_nn(stacked_t.T, weights)
    half = projected.shape[0] // 2
    out[0] = projected[:half]
    out[1] = projected[half:]
    store.wait()
    for copy in sent + gathers:
        copy.wait_send()


def shards(sizes, density, velocity, pressure, start_block, test_vectors):
    nz, ny, nm = sizes
    slots = max(2 * ny, nz, 2 * nm)
    anywhere = pl.BlockSpec(memory_space=pl.ANY)
    f32 = jnp.float32
    samples = test_vectors.shape[0] * test_vectors.shape[1]
    return pl.pallas_call(
        functools.partial(window_kernel, nz, ny, nm),
        out_shape=(
            jax.ShapeDtypeStruct((1, 5, *density.shape[1:]), f32),
            jax.ShapeDtypeStruct(test_vectors.shape, f32),
        ),
        in_specs=[anywhere] * 5,
        out_specs=(anywhere, pl.BlockSpec(memory_space=pltpu.VMEM)),
        scratch_shapes=[
            pltpu.VMEM((10, PLANES, ROWS, 256), f32),
            pltpu.VMEM((10, PLANES, ROWS, 256), f32),
            pltpu.VMEM((5, PLANES, ROWS, 256), f32),
            pltpu.VMEM((5, 4, OWN_ROWS, 256), f32),
            pltpu.VMEM((2, 5, 8, 256), f32),
            pltpu.VMEM((2, 5, 8, 256), f32),
            pltpu.VMEM((4, 8, 256), f32),
            pltpu.VMEM((4, 8, 256), f32),
            pltpu.VMEM((256, 128), f32),
            pltpu.VMEM((4, OWN_ROWS, 128), f32),
            pltpu.VMEM(start_block.shape[1:], f32),
            pltpu.VMEM(test_vectors.shape, f32),
            pltpu.VMEM((nm, samples, 128), f32),
            pltpu.VMEM((2, 8, 128), f32),
            pltpu.VMEM((2 * ny, 8, 128), f32),
            pltpu.VMEM((nz, 8, 128), f32),
            pltpu.VMEM((2 * nm, 8, 128), f32),
            pltpu.VMEM((2, 8, 256), f32),
            pltpu.VMEM((2 * ny, 8, 256), f32),
            pltpu.VMEM((nz, 8, 256), f32),
            pltpu.VMEM((2 * nm, 8, 256), f32),
            pltpu.SemaphoreType.DMA((6,)),
            pltpu.SemaphoreType.DMA((2, 10)),
            pltpu.SemaphoreType.DMA((2, 3, 2, slots)),
            pltpu.SemaphoreType.DMA((2, nm)),
        ],
        compiler_params=pltpu.CompilerParams(
            collective_id=0, has_side_effects=True, vmem_limit_bytes=48 * 1024 * 1024
        ),
    )(density, velocity, pressure, start_block, test_vectors)


def solution(mesh):
    sizes = (mesh.shape["gx"] // 2, mesh.shape["gy"], mesh.shape["member"])
    return jax.shard_map(
        functools.partial(shards, sizes),
        mesh=mesh,
        in_specs=(
            P("member", "gx", "gy", None),
            P("member", None, "gx", "gy", None),
            P("member", "gx", "gy", None),
            P("member", None, None),
            P("gx", "gy", None),
        ),
        out_specs=(P("member", None, "gx", "gy", None), P("gx", "gy", None)),
        check_vma=False,
    )
```

time: 82.5 us -> 54.7 us (0.66)
  starting transfers between devices: 12.2 us -> 0 us
  waiting for transfers between devices: 9.8 us -> 0 us
  other arithmetic: 8.3 us -> 0 us
  Pallas kernels: 43.3 us -> 48.8 us
  local copies, waits for them, and re-layouts: 7.5 us -> 5.05 us
    ppermute x8 -> x0, starting transfers between devices: 12.2 us -> none  [the longest x4 6.75 us: padded(): lax.ppermute(lax.slice_in_dim(block, block.shape[dim] - width, None, axis...]
    ppermute x8 -> x0, waiting for transfers between devices: 9.8 us -> none  [the longest x4 5.2 us: padded(): lax.ppermute(lax.slice_in_dim(block, block.shape[dim] - width, None, axis...]
    slice x19 -> x0, local copies, waits for them, and re-layouts: 5.82 us -> none  [the longest x6 2.48 us: tendency(): right_fields = jnp.roll(fields, -1, axis=3)]
    pallas_call x1, Pallas kernels: 43.3 us -> 48.8 us  [shards(): pl.pallas_call(functools.partial(window_kernel, nz, ny, nm), out_shape=(j...]
    unnamed x11, local copies, waits for them, and re-layouts: 1.41 us -> 5.05 us
    sub x6 -> x0, other arithmetic: 2.7 us -> none  [tendency(): 0.5 * (left_flux + right_flux)]
    add x7 -> x0, other arithmetic: 2.55 us -> none  [the longest x1 1 us: conserved(): pressure / (HEAT_RATIO - 1.0)]
    mul x5 -> x0, other arithmetic: 1.23 us -> none  [the longest x1 1.12 us: conserved(): momentum = density[None] * velocity]
  transfers between devices with their start and end apart: 8 -> 0, of which waited for: 6 -> 0; matrix products, arithmetic and copies ran while one was open for 0% -> 0% of each run, Pallas kernels for 0% -> 0%
where the time goes in v2:
time: 54.7 us; the launch traced here: 54.5 us
  Pallas kernels  48.8 us (89%)
  local copies, waits for them, and re-layouts  5.05 us (9%)
  between operations  0.66 us (1%)
    pallas_call x1, Pallas kernels, shards(): pl.pallas_call(functools.partial(window_kernel, nz, ny, nm), out_shape=(j...  48.8 us
    unnamed x11, local copies, waits for them, and re-layouts  5.05 us

profile of v2, /device:TPU:1, one launch (start us, length us, event | category | flops | bytes accessed | tf_op | source)
XLA Modules:
  0.0 54.5 jit_solution(18423216366621375540)
XLA Ops:
  0.6 0.0 copy-start.3
  0.6 0.8 %copy.7.block = f32[1,128,16]{2,1,0:T(8,128)S(1)} copy(f32[1,128,16]{1,2,0:T(8,128)} %param.8) | data formatting | bytes 16384 | tf_op args[3]
  1.4 0.0 copy-done.3
  1.4 0.0 copy-start
  1.5 1.0 %copy-done = f32[1,3,4,32,256]{4,3,2,1,0:T(8,128)S(1)} copy-done((f32[1,3,4,32,256]{4,3,2,1,0:T(8,128)S(1)}, f32[1,3,4,32,256]{4,3,2,1,0:T(8,128)}, u32[]{:S(2)}) %copy-start) | copy-done | bytes 393240
  2.4 0.0 copy-start.1
  2.4 0.9 %copy-done.1 = f32[1,4,32,256]{3,2,1,0:T(8,128)S(1)} copy-done((f32[1,4,32,256]{3,2,1,0:T(8,128)S(1)}, f32[1,4,32,256]{3,2,1,0:T(8,128)}, u32[]{:S(2)}) %copy-start.1) | copy-done | bytes 131096
  3.4 0.0 copy-start.2
  3.4 0.9 %copy-done.2 = f32[1,4,32,256]{3,2,1,0:T(8,128)S(1)} copy-done((f32[1,4,32,256]{3,2,1,0:T(8,128)S(1)}, f32[1,4,32,256]{3,2,1,0:T(8,128)}, u32[]{:S(2)}) %copy-start.2) | copy-done | bytes 131096
  4.3 48.8 %shard_map.68 = (f32[1,5,4,32,256]{4,3,2,1,0:T(8,128)S(1)}, f32[2,16,128]{2,1,0:T(8,128)S(1)}) custom-call(f32[1,4,32,256]{3,2,1,0:T(8,128)S(1)} %copy-done.1, f32[1,3,4,32,256]{4,3,2,1,0:T(8,128)S(1)} %copy-done, f32[1,4,32,256]{3,2,1,0:T(8,128)S(1)} %copy-done.2, f32[1,128,16]{2,1,0:T(8,128)S(1)} %copy.7.block, f32[2,16,128]{2,1,0:T(8,128)S(1)} %copy-done.3), custom_call_target="tpu_custom_call" | custom-call | tf_op jit(solution)/shard_map/pallas_call | solution.py:434
  53.0 0.8 %copy.10 = f32[1,5,4,32,256]{4,3,2,1,0:T(8,128)} copy(f32[1,5,4,32,256]{4,3,2,1,0:T(8,128)S(1)} %get-tuple-element.4) | data formatting | bytes 1310720
  53.9 0.6 %copy.11 = f32[2,16,128]{2,1,0:T(8,128)} copy(f32[2,16,128]{2,1,0:T(8,128)S(1)} %get-tuple-element.5) | data formatting | bytes 32768
Async XLA Ops:
  0.6 0.8 %copy-start.3 = (f32[2,16,128]{2,1,0:T(8,128)S(1)}, f32[2,16,128]{2,1,0:T(8,128)}, u32[]{:S(2)}) copy-start(f32[2,16,128]{2,1,0:T(8,128)} %test.1) | copy-start | bytes 49156
  1.4 1.0 %copy-start = (f32[1,3,4,32,256]{4,3,2,1,0:T(8,128)S(1)}, f32[1,3,4,32,256]{4,3,2,1,0:T(8,128)}, u32[]{:S(2)}) copy-start(f32[1,3,4,32,256]{4,3,2,1,0:T(8,128)} %velocity.1) | copy-start | bytes 1179652
  2.4 0.9 %copy-start.1 = (f32[1,4,32,256]{3,2,1,0:T(8,128)S(1)}, f32[1,4,32,256]{3,2,1,0:T(8,128)}, u32[]{:S(2)}) copy-start(f32[1,4,32,256]{3,2,1,0:T(8,128)} %density.1) | copy-start | bytes 393220
  3.4 0.9 %copy-start.2 = (f32[1,4,32,256]{3,2,1,0:T(8,128)S(1)}, f32[1,4,32,256]{3,2,1,0:T(8,128)}, u32[]{:S(2)}) copy-start(f32[1,4,32,256]{3,2,1,0:T(8,128)} %pressure.1) | copy-start | bytes 393220

commit v3 on v2

--- a/solution.py
+++ b/solution.py
@@ -243,8 +243,7 @@
     local_sems, halo_sems, sems, member_sems,
 ):
     place = Place(nz, ny, nm)
-    rank = block.shape[2]
-    snaps = block.shape[1]
+    rank, snaps = block.shape[1:]
     barrier = pltpu.get_barrier_semaphore()
     peers = place.everyone()
     own = pl.ds(0, OWN_ROWS)
@@ -357,7 +356,7 @@
     matrix_all[place.m] = matrix
     for copy in late_loads:
         copy.wait()
-    fold = dot_nn(dot_nt(block_in[...].T, matrix), matrix)
+    fold = dot_nn(dot_nt(block_in[...], matrix), matrix)
     fold_half[0] = fold[:8]
     fold_half[1] = fold[8:]
     gathers = [
@@ -428,8 +427,9 @@
 def shards(sizes, density, velocity, pressure, start_block, test_vectors):
     nz, ny, nm = sizes
     slots = max(2 * ny, nz, 2 * nm)
-    anywhere = pl.BlockSpec(memory_space=pl.ANY)
+    in_hbm = pl.BlockSpec(memory_space=pltpu.HBM)
     f32 = jnp.float32
+    block_t = jnp.swapaxes(start_block, 1, 2)
     samples = test_vectors.shape[0] * test_vectors.shape[1]
     return pl.pallas_call(
         functools.partial(window_kernel, nz, ny, nm),
@@ -437,8 +437,8 @@
             jax.ShapeDtypeStruct((1, 5, *density.shape[1:]), f32),
             jax.ShapeDtypeStruct(test_vectors.shape, f32),
         ),
-        in_specs=[anywhere] * 5,
-        out_specs=(anywhere, pl.BlockSpec(memory_space=pltpu.VMEM)),
+        in_specs=[in_hbm] * 5,
+        out_specs=(in_hbm, pl.BlockSpec(memory_space=pltpu.VMEM)),
         scratch_shapes=[
             pltpu.VMEM((10, PLANES, ROWS, 256), f32),
             pltpu.VMEM((10, PLANES, ROWS, 256), f32),
@@ -450,7 +450,7 @@
             pltpu.VMEM((4, 8, 256), f32),
             pltpu.VMEM((256, 128), f32),
             pltpu.VMEM((4, OWN_ROWS, 128), f32),
-            pltpu.VMEM(start_block.shape[1:], f32),
+            pltpu.VMEM(block_t.shape[1:], f32),
             pltpu.VMEM(test_vectors.shape, f32),
             pltpu.VMEM((nm, samples, 128), f32),
             pltpu.VMEM((2, 8, 128), f32),
@@ -469,7 +469,7 @@
         compiler_params=pltpu.CompilerParams(
             collective_id=0, has_side_effects=True, vmem_limit_bytes=48 * 1024 * 1024
         ),
-    )(density, velocity, pressure, start_block, test_vectors)
+    )(density, velocity, pressure, block_t, test_vectors)
 
 
 def solution(mesh):

time: 54.7 us -> 55.2 us (level)
  local copies, waits for them, and re-layouts: 5.05 us -> 5.65 us
    unnamed x11 -> x12, local copies, waits for them, and re-layouts: 5.05 us -> 5.65 us
where the time goes in v3:
time: 55.2 us; the launch traced here: 54.9 us
  Pallas kernels  48.6 us (88%)
  local copies, waits for them, and re-layouts  5.65 us (10%)
  between operations  0.65 us (1%)
    pallas_call x1, Pallas kernels, shards(): pl.pallas_call(functools.partial(window_kernel, nz, ny, nm), out_shape=(j...  48.6 us
    unnamed x12, local copies, waits for them, and re-layouts  5.65 us

profile of v3, /device:TPU:1, one launch (start us, length us, event | category | flops | bytes accessed | tf_op | source)
XLA Modules:
  0.0 54.9 jit_solution(15518149085099119138)
XLA Ops:
  0.6 0.0 copy-start
  0.6 1.0 %copy-done = f32[1,3,4,32,256]{4,3,2,1,0:T(8,128)S(1)} copy-done((f32[1,3,4,32,256]{4,3,2,1,0:T(8,128)S(1)}, f32[1,3,4,32,256]{4,3,2,1,0:T(8,128)}, u32[]{:S(2)}) %copy-start) | copy-done | bytes 393240
  1.6 0.0 copy-start.1
  1.6 0.9 %copy-done.1 = f32[1,4,32,256]{3,2,1,0:T(8,128)S(1)} copy-done((f32[1,4,32,256]{3,2,1,0:T(8,128)S(1)}, f32[1,4,32,256]{3,2,1,0:T(8,128)}, u32[]{:S(2)}) %copy-start.1) | copy-done | bytes 131096
  2.5 0.0 copy-start.2
  2.5 0.9 %copy-done.2 = f32[1,4,32,256]{3,2,1,0:T(8,128)S(1)} copy-done((f32[1,4,32,256]{3,2,1,0:T(8,128)S(1)}, f32[1,4,32,256]{3,2,1,0:T(8,128)}, u32[]{:S(2)}) %copy-start.2) | copy-done | bytes 131096
  3.4 0.0 copy-start.3
  3.4 0.7 %copy-done.3 = f32[2,16,128]{2,1,0:T(8,128)S(1)} copy-done((f32[2,16,128]{2,1,0:T(8,128)S(1)}, f32[2,16,128]{2,1,0:T(8,128)}, u32[]{:S(2)}) %copy-start.3) | copy-done | bytes 16408
  4.2 0.0 copy-start.4
  4.2 0.7 %copy-done.4 = f32[1,128,16]{1,2,0:T(8,128)S(1)} copy-done((f32[1,128,16]{1,2,0:T(8,128)S(1)}, f32[1,128,16]{1,2,0:T(8,128)}, u32[]{:S(2)}) %copy-start.4) | copy-done | bytes 8216
  4.9 48.6 %shard_map.68 = (f32[1,5,4,32,256]{4,3,2,1,0:T(8,128)S(1)}, f32[2,16,128]{2,1,0:T(8,128)S(1)}) custom-call(f32[1,4,32,256]{3,2,1,0:T(8,128)S(1)} %copy-done.1, f32[1,3,4,32,256]{4,3,2,1,0:T(8,128)S(1)} %copy-done, f32[1,4,32,256]{3,2,1,0:T(8,128)S(1)} %copy-done.2, f32[1,16,128]{2,1,0:T(8,128)S(1)} %bitcast.1, f32[2,16,128]{2,1,0:T(8,128)S(1)} %copy-done.3), custom_call_target="tpu_custom_call" | custom-call | tf_op jit(solution)/shard_map/pallas_call | solution.py:434
  53.5 0.8 %copy.9 = f32[1,5,4,32,256]{4,3,2,1,0:T(8,128)} copy(f32[1,5,4,32,256]{4,3,2,1,0:T(8,128)S(1)} %get-tuple-element.4) | data formatting | bytes 1310720
  54.3 0.6 %copy.10 = f32[2,16,128]{2,1,0:T(8,128)} copy(f32[2,16,128]{2,1,0:T(8,128)S(1)} %get-tuple-element.5) | data formatting | bytes 32768
Async XLA Ops:
  0.6 1.0 %copy-start = (f32[1,3,4,32,256]{4,3,2,1,0:T(8,128)S(1)}, f32[1,3,4,32,256]{4,3,2,1,0:T(8,128)}, u32[]{:S(2)}) copy-start(f32[1,3,4,32,256]{4,3,2,1,0:T(8,128)} %velocity.1) | copy-start | bytes 1179652
  1.6 0.9 %copy-start.1 = (f32[1,4,32,256]{3,2,1,0:T(8,128)S(1)}, f32[1,4,32,256]{3,2,1,0:T(8,128)}, u32[]{:S(2)}) copy-start(f32[1,4,32,256]{3,2,1,0:T(8,128)} %density.1) | copy-start | bytes 393220
  2.5 0.9 %copy-start.2 = (f32[1,4,32,256]{3,2,1,0:T(8,128)S(1)}, f32[1,4,32,256]{3,2,1,0:T(8,128)}, u32[]{:S(2)}) copy-start(f32[1,4,32,256]{3,2,1,0:T(8,128)} %pressure.1) | copy-start | bytes 393220
  3.4 0.7 %copy-start.3 = (f32[2,16,128]{2,1,0:T(8,128)S(1)}, f32[2,16,128]{2,1,0:T(8,128)}, u32[]{:S(2)}) copy-start(f32[2,16,128]{2,1,0:T(8,128)} %test.1) | copy-start | bytes 49156
  4.2 0.7 %copy-start.4 = (f32[1,128,16]{1,2,0:T(8,128)S(1)}, f32[1,128,16]{1,2,0:T(8,128)}, u32[]{:S(2)}) copy-start(f32[1,128,16]{1,2,0:T(8,128)} %param.8) | copy-start | bytes 24580

commit v4 on v2

--- a/solution.py
+++ b/solution.py
@@ -136,16 +136,26 @@
     return first + second + third
 
 
+PANEL = 4
+
+
 def eliminate(gram, cross):
-    size = gram.shape[0]
-    rows = lax.broadcasted_iota(jnp.int32, (size, 1), 0)
-    scale = jnp.ones((size, 1), jnp.float32)
-    for k in range(size):
-        inverse = 1.0 / gram[k : k + 1, k : k + 1]
-        factor = jnp.where(rows == k, 0.0, gram[:, k : k + 1] * inverse)
-        scale = jnp.where(rows == k, inverse, scale)
-        cross = cross - factor * cross[k : k + 1]
-        gram = gram - factor * gram[k : k + 1]
+    size, lanes = cross.shape
+    rows = lax.broadcasted_iota(jnp.int32, (size, lanes), 0)
+    scale = jnp.ones((size, lanes), jnp.float32)
+    for first in range(0, size, PANEL):
+        columns = [
+            jnp.broadcast_to(gram[:, k : k + 1], (size, lanes)) for k in range(first, first + PANEL)
+        ]
+        for at in range(PANEL):
+            k = first + at
+            inverse = 1.0 / columns[at][k : k + 1]
+            factor = jnp.where(rows == k, 0.0, columns[at] * inverse)
+            scale = jnp.where(rows == k, inverse, scale)
+            for later in range(at + 1, PANEL):
+                columns[later] = columns[later] - factor * columns[later][k : k + 1]
+            cross = cross - factor * cross[k : k + 1]
+            gram = gram - factor * gram[k : k + 1]
     return cross * scale
 
 

time: 54.7 us -> 52.1 us (0.952)
  Pallas kernels: 48.8 us -> 46.2 us
    pallas_call x1, Pallas kernels: 48.8 us -> 46.2 us  [shards(): pl.pallas_call(functools.partial(window_kernel, nz, ny, nm), out_shape=(j...]
where the time goes in v4:
time: 52.1 us; the launch traced here: 51.9 us
  Pallas kernels  46.2 us (89%)
  local copies, waits for them, and re-layouts  5.05 us (10%)
  between operations  0.66 us (1%)
    pallas_call x1, Pallas kernels, shards(): pl.pallas_call(functools.partial(window_kernel, nz, ny, nm), out_shape=(j...  46.2 us
    unnamed x11, local copies, waits for them, and re-layouts  5.05 us

profile of v4, /device:TPU:1, one launch (start us, length us, event | category | flops | bytes accessed | tf_op | source)
XLA Modules:
  0.0 51.9 jit_solution(11129609539981191674)
XLA Ops:
  0.6 0.0 copy-start.3
  0.6 0.8 %copy.7.block = f32[1,128,16]{2,1,0:T(8,128)S(1)} copy(f32[1,128,16]{1,2,0:T(8,128)} %param.8) | data formatting | bytes 16384 | tf_op args[3]
  1.4 0.0 copy-done.3
  1.4 0.0 copy-start
  1.5 1.0 %copy-done = f32[1,3,4,32,256]{4,3,2,1,0:T(8,128)S(1)} copy-done((f32[1,3,4,32,256]{4,3,2,1,0:T(8,128)S(1)}, f32[1,3,4,32,256]{4,3,2,1,0:T(8,128)}, u32[]{:S(2)}) %copy-start) | copy-done | bytes 393240
  2.4 0.0 copy-start.1
  2.4 0.9 %copy-done.1 = f32[1,4,32,256]{3,2,1,0:T(8,128)S(1)} copy-done((f32[1,4,32,256]{3,2,1,0:T(8,128)S(1)}, f32[1,4,32,256]{3,2,1,0:T(8,128)}, u32[]{:S(2)}) %copy-start.1) | copy-done | bytes 131096
  3.4 0.0 copy-start.2
  3.4 0.9 %copy-done.2 = f32[1,4,32,256]{3,2,1,0:T(8,128)S(1)} copy-done((f32[1,4,32,256]{3,2,1,0:T(8,128)S(1)}, f32[1,4,32,256]{3,2,1,0:T(8,128)}, u32[]{:S(2)}) %copy-start.2) | copy-done | bytes 131096
  4.3 46.2 %shard_map.68 = (f32[1,5,4,32,256]{4,3,2,1,0:T(8,128)S(1)}, f32[2,16,128]{2,1,0:T(8,128)S(1)}) custom-call(f32[1,4,32,256]{3,2,1,0:T(8,128)S(1)} %copy-done.1, f32[1,3,4,32,256]{4,3,2,1,0:T(8,128)S(1)} %copy-done, f32[1,4,32,256]{3,2,1,0:T(8,128)S(1)} %copy-done.2, f32[1,128,16]{2,1,0:T(8,128)S(1)} %copy.7.block, f32[2,16,128]{2,1,0:T(8,128)S(1)} %copy-done.3), custom_call_target="tpu_custom_call" | custom-call | tf_op jit(solution)/shard_map/pallas_call | solution.py:444
  50.4 0.8 %copy.10 = f32[1,5,4,32,256]{4,3,2,1,0:T(8,128)} copy(f32[1,5,4,32,256]{4,3,2,1,0:T(8,128)S(1)} %get-tuple-element.4) | data formatting | bytes 1310720
  51.3 0.6 %copy.11 = f32[2,16,128]{2,1,0:T(8,128)} copy(f32[2,16,128]{2,1,0:T(8,128)S(1)} %get-tuple-element.5) | data formatting | bytes 32768
Async XLA Ops:
  0.6 0.8 %copy-start.3 = (f32[2,16,128]{2,1,0:T(8,128)S(1)}, f32[2,16,128]{2,1,0:T(8,128)}, u32[]{:S(2)}) copy-start(f32[2,16,128]{2,1,0:T(8,128)} %test.1) | copy-start | bytes 49156
  1.4 1.0 %copy-start = (f32[1,3,4,32,256]{4,3,2,1,0:T(8,128)S(1)}, f32[1,3,4,32,256]{4,3,2,1,0:T(8,128)}, u32[]{:S(2)}) copy-start(f32[1,3,4,32,256]{4,3,2,1,0:T(8,128)} %velocity.1) | copy-start | bytes 1179652
  2.4 0.9 %copy-start.1 = (f32[1,4,32,256]{3,2,1,0:T(8,128)S(1)}, f32[1,4,32,256]{3,2,1,0:T(8,128)}, u32[]{:S(2)}) copy-start(f32[1,4,32,256]{3,2,1,0:T(8,128)} %density.1) | copy-start | bytes 393220
  3.4 0.9 %copy-start.2 = (f32[1,4,32,256]{3,2,1,0:T(8,128)S(1)}, f32[1,4,32,256]{3,2,1,0:T(8,128)}, u32[]{:S(2)}) copy-start(f32[1,4,32,256]{3,2,1,0:T(8,128)} %pressure.1) | copy-start | bytes 393220

commit v5 on v4

--- a/solution.py
+++ b/solution.py
@@ -136,7 +136,7 @@
     return first + second + third
 
 
-PANEL = 4
+PANEL = 8
 
 
 def eliminate(gram, cross):

time: 52.1 us -> 51 us (0.979)
  Pallas kernels: 46.2 us -> 45.1 us
    pallas_call x1, Pallas kernels: 46.2 us -> 45.1 us  [shards(): pl.pallas_call(functools.partial(window_kernel, nz, ny, nm), out_shape=(j...]
where the time goes in v5:
time: 51 us; the launch traced here: 50.8 us
  Pallas kernels  45.1 us (88%)
  local copies, waits for them, and re-layouts  5.05 us (10%)
  between operations  0.66 us (1%)
    pallas_call x1, Pallas kernels, shards(): pl.pallas_call(functools.partial(window_kernel, nz, ny, nm), out_shape=(j...  45.1 us
    unnamed x11, local copies, waits for them, and re-layouts  5.05 us

profile of v5, /device:TPU:1, one launch (start us, length us, event | category | flops | bytes accessed | tf_op | source)
XLA Modules:
  0.0 50.8 jit_solution(5700143450689038004)
XLA Ops:
  0.6 0.0 copy-start.3
  0.6 0.8 %copy.7.block = f32[1,128,16]{2,1,0:T(8,128)S(1)} copy(f32[1,128,16]{1,2,0:T(8,128)} %param.8) | data formatting | bytes 16384 | tf_op args[3]
  1.4 0.0 copy-done.3
  1.4 0.0 copy-start
  1.5 1.0 %copy-done = f32[1,3,4,32,256]{4,3,2,1,0:T(8,128)S(1)} copy-done((f32[1,3,4,32,256]{4,3,2,1,0:T(8,128)S(1)}, f32[1,3,4,32,256]{4,3,2,1,0:T(8,128)}, u32[]{:S(2)}) %copy-start) | copy-done | bytes 393240
  2.4 0.0 copy-start.1
  2.4 0.9 %copy-done.1 = f32[1,4,32,256]{3,2,1,0:T(8,128)S(1)} copy-done((f32[1,4,32,256]{3,2,1,0:T(8,128)S(1)}, f32[1,4,32,256]{3,2,1,0:T(8,128)}, u32[]{:S(2)}) %copy-start.1) | copy-done | bytes 131096
  3.4 0.0 copy-start.2
  3.4 0.9 %copy-done.2 = f32[1,4,32,256]{3,2,1,0:T(8,128)S(1)} copy-done((f32[1,4,32,256]{3,2,1,0:T(8,128)S(1)}, f32[1,4,32,256]{3,2,1,0:T(8,128)}, u32[]{:S(2)}) %copy-start.2) | copy-done | bytes 131096
  4.3 45.1 %shard_map.68 = (f32[1,5,4,32,256]{4,3,2,1,0:T(8,128)S(1)}, f32[2,16,128]{2,1,0:T(8,128)S(1)}) custom-call(f32[1,4,32,256]{3,2,1,0:T(8,128)S(1)} %copy-done.1, f32[1,3,4,32,256]{4,3,2,1,0:T(8,128)S(1)} %copy-done, f32[1,4,32,256]{3,2,1,0:T(8,128)S(1)} %copy-done.2, f32[1,128,16]{2,1,0:T(8,128)S(1)} %copy.7.block, f32[2,16,128]{2,1,0:T(8,128)S(1)} %copy-done.3), custom_call_target="tpu_custom_call" | custom-call | tf_op jit(solution)/shard_map/pallas_call | solution.py:444
  49.3 0.8 %copy.10 = f32[1,5,4,32,256]{4,3,2,1,0:T(8,128)} copy(f32[1,5,4,32,256]{4,3,2,1,0:T(8,128)S(1)} %get-tuple-element.4) | data formatting | bytes 1310720
  50.2 0.6 %copy.11 = f32[2,16,128]{2,1,0:T(8,128)} copy(f32[2,16,128]{2,1,0:T(8,128)S(1)} %get-tuple-element.5) | data formatting | bytes 32768
Async XLA Ops:
  0.6 0.8 %copy-start.3 = (f32[2,16,128]{2,1,0:T(8,128)S(1)}, f32[2,16,128]{2,1,0:T(8,128)}, u32[]{:S(2)}) copy-start(f32[2,16,128]{2,1,0:T(8,128)} %test.1) | copy-start | bytes 49156
  1.4 1.0 %copy-start = (f32[1,3,4,32,256]{4,3,2,1,0:T(8,128)S(1)}, f32[1,3,4,32,256]{4,3,2,1,0:T(8,128)}, u32[]{:S(2)}) copy-start(f32[1,3,4,32,256]{4,3,2,1,0:T(8,128)} %velocity.1) | copy-start | bytes 1179652
  2.4 0.9 %copy-start.1 = (f32[1,4,32,256]{3,2,1,0:T(8,128)S(1)}, f32[1,4,32,256]{3,2,1,0:T(8,128)}, u32[]{:S(2)}) copy-start(f32[1,4,32,256]{3,2,1,0:T(8,128)} %density.1) | copy-start | bytes 393220
  3.4 0.9 %copy-start.2 = (f32[1,4,32,256]{3,2,1,0:T(8,128)S(1)}, f32[1,4,32,256]{3,2,1,0:T(8,128)}, u32[]{:S(2)}) copy-start(f32[1,4,32,256]{3,2,1,0:T(8,128)} %pressure.1) | copy-start | bytes 393220
